TPU v7x, 256 devices: a whole 4x4x8 slice. The times are simulated.
256 devices in a mesh: dp: 32 (over z, y), seq: 8 (over x, core).
Axes of the slice: x: 4, y: 4, z: 8, core: 2. Of those that a mesh axis runs over, the one named last changes fastest.
Arguments:
- slot_tokens: bfloat16 [416, 512, 1152], P('dp', 'seq'), may hold values from -12 to 12
- modulation: float32 [32, 6, 1152], P('dp'), may hold values from -2.5 to 2.5
- counts: int32 [32], replicated, may hold values from 1 to 13, as said below
- dest: int32 [32, 13], replicated, may hold values from 0 to 223, as said below
- qkv_spatial: bfloat16 [1152, 1728], replicated, may hold values from -4 to 4
- out_spatial: bfloat16 [576, 1152], replicated, may hold values from -0.25 to 0.25
- qkv_temporal: bfloat16 [1152, 1728], replicated, may hold values from -4 to 4
- out_temporal: bfloat16 [576, 1152], replicated, may hold values from -0.25 to 0.25
Outputs:
- video_out: bfloat16 [224, 512, 1152], P('dp', 'seq')
Inputs may be any that keep to these rules, and one draw needn't show every extreme that they name: Group g holds blocks in slots 0 to counts[g] - 1; the counts sum to 224; some group holds 13 blocks. Over the slots q below counts[g] of all groups g, dest[g, q] takes every value 0 to 223 exactly once; one group sends at most 1 block to one video, and some group sends 1; entries at slots from counts[g] on are arbitrary values of the same range.
All inputs are finite; a program needn't handle non-finite values.
Results may differ from a plain program's by a relative error of at most 0.0057.
Values may be sent and summed in bfloat16 or wider, within the bound.
No kernel may reach another device: no remote copies, remote signals or barrier semaphores. Data moves between devices by JAX's collectives and lax.ppermute only.
A program may use at most 64 MiB of HBM per device.

v0:
```python
import math
import jax
import jax.numpy as jnp
from jax import lax
from jax.sharding import PartitionSpec as P

HEADS = 8
HEAD_DIM = 72
NFD = 7
epsilon = 1e-06


def norm_mod(tokens, shift_row, scale_row):
    values = tokens.astype(jnp.float32)
    center = values - jnp.mean(values, axis=-1, keepdims=True)
    spread = jnp.mean(center * center, axis=-1, keepdims=True)
    return (center * lax.rsqrt(spread + epsilon) * (1.0 + scale_row) + shift_row).astype(
        jnp.bfloat16
    )


def attention(qkv_rows, batch_count, length):
    parts = qkv_rows.reshape(batch_count, length, 3, HEADS, HEAD_DIM)
    factor = 1.0 / math.sqrt(HEAD_DIM)
    scores = (
        jnp.einsum(
            "bqhs,bkhs->bhqk", parts[:, :, 0], parts[:, :, 1], preferred_element_type=jnp.float32
        )
        * factor
    )
    highest = jnp.max(scores, axis=-1, keepdims=True)
    raised = jnp.exp(scores - highest)
    weights = (raised / jnp.sum(raised, axis=-1, keepdims=True)).astype(jnp.bfloat16)
    mixed = jnp.einsum(
        "bhqk,bkhs->bqhs", weights, parts[:, :, 2], preferred_element_type=jnp.float32
    )
    return mixed.astype(jnp.bfloat16).reshape(batch_count * length, HEADS * HEAD_DIM)


def spatial_block(frames, modulation_rows, w_qkv, w_out):
    frame_count, patch_count, model_width = frames.shape
    shift_rows = modulation_rows[:, 0][:, None, :]
    scale_rows = modulation_rows[:, 1][:, None, :]
    gate_rows = modulation_rows[:, 2][:, None, :]
    normed = norm_mod(frames, shift_rows, scale_rows)
    qkv_rows = jnp.dot(
        normed.reshape(-1, model_width), w_qkv, preferred_element_type=jnp.float32
    ).astype(jnp.bfloat16)
    mixed = attention(qkv_rows, frame_count, patch_count)
    projected = jnp.dot(mixed, w_out, preferred_element_type=jnp.float32).reshape(
        frame_count, patch_count, model_width
    )
    return (frames.astype(jnp.float32) + gate_rows * projected).astype(jnp.bfloat16)


def on_device(
    slot_tokens, modulation, counts, dest, qkv_spatial, out_spatial, qkv_temporal, out_temporal
):
    group_count = lax.axis_size("dp")
    slot_count, patch_count, model_width = slot_tokens.shape
    block_count = NFD
    send_room = (slot_count + group_count - 1) // group_count
    group_index = lax.axis_index("dp")
    slot_ids = jnp.arange(slot_count, dtype=jnp.int32)
    group_ids = jnp.arange(group_count, dtype=jnp.int32)
    room_ids = jnp.arange(send_room, dtype=jnp.int32)
    live_slots = slot_ids[None, :] < counts[:, None]
    target_group = dest // block_count
    earlier = slot_ids[:, None] < slot_ids[None, :]
    same_target = (
        live_slots[:, :, None]
        & (target_group[:, :, None] == target_group[:, None, :])
        & earlier[None, :, :]
    )
    send_rank = jnp.sum(same_target.astype(jnp.int32), axis=1)
    own_live = lax.dynamic_index_in_dim(
        live_slots.astype(jnp.int32), group_index, 0, keepdims=False
    )
    own_target = lax.dynamic_index_in_dim(target_group, group_index, 0, keepdims=False)
    own_rank = lax.dynamic_index_in_dim(send_rank, group_index, 0, keepdims=False)
    picks = (
        (own_live[:, None, None] > 0)
        & (own_target[:, None, None] == group_ids[None, :, None])
        & (own_rank[:, None, None] == room_ids[None, None, :])
    )
    chosen_slot = jnp.sum(picks.astype(jnp.int32) * slot_ids[:, None, None], axis=0).reshape(-1)
    video_rows = lax.all_gather(modulation, "dp", axis=0, tiled=True)
    slot_modulation = jnp.take(video_rows, own_target, axis=0)
    processed = spatial_block(slot_tokens, slot_modulation, qkv_spatial, out_spatial)
    payload = jnp.take(processed, chosen_slot, axis=0)
    arrived = lax.all_to_all(payload, "dp", split_axis=0, concat_axis=0, tiled=True)
    wanted = group_index * block_count + jnp.arange(block_count, dtype=jnp.int32)
    matches = (live_slots[:, :, None] & (dest[:, :, None] == wanted[None, None, :])).astype(
        jnp.int32
    )
    source_group = jnp.sum(matches * group_ids[:, None, None], axis=(0, 1))
    source_rank = jnp.sum(matches * send_rank[:, :, None], axis=(0, 1))
    placed = jnp.take(arrived, source_group * send_room + source_rank, axis=0)
    own_modulation = modulation[0]
    shard_count = lax.axis_size("seq")
    widest = patch_count // shard_count
    frame_total = shard_count * block_count
    channels = placed.shape[-1]
    selected = placed.reshape(block_count, shard_count, widest, channels)
    moved = lax.all_to_all(selected, "seq", split_axis=1, concat_axis=0, tiled=True)
    token_rows = moved.reshape(frame_total * widest, channels)
    normed_rows = norm_mod(token_rows, own_modulation[3], own_modulation[4])
    qkv_rows = jnp.dot(normed_rows, qkv_temporal, preferred_element_type=jnp.float32).astype(
        jnp.bfloat16
    )
    qkv_width = qkv_rows.shape[-1]
    by_patch = (
        qkv_rows.reshape(frame_total, widest, qkv_width)
        .transpose(1, 0, 2)
        .reshape(widest * frame_total, qkv_width)
    )
    mixed = attention(by_patch, widest, frame_total)
    attn_width = mixed.shape[-1]
    mixed = (
        mixed.reshape(widest, frame_total, attn_width)
        .transpose(1, 0, 2)
        .reshape(frame_total * widest, attn_width)
    )
    projected_rows = jnp.dot(mixed, out_temporal, preferred_element_type=jnp.float32)
    homeward = (token_rows.astype(jnp.float32) + own_modulation[5] * projected_rows).astype(
        jnp.bfloat16
    )
    back_width = homeward.shape[-1]
    returned = lax.all_to_all(
        homeward.reshape(frame_total, 1, widest, back_width),
        "seq",
        split_axis=0,
        concat_axis=1,
        tiled=True,
    )
    restored = returned.reshape(block_count, patch_count, back_width)
    return restored


def solution(mesh):
    in_specs = (P("dp", "seq", None), P("dp", None, None), P(), P(), P(), P(), P(), P())
    out_specs = P("dp", "seq", None)
    return jax.shard_map(
        on_device, mesh=mesh, in_specs=in_specs, out_specs=out_specs, check_vma=False
    )
```

profile of v0, /device:TPU:1, one launch (start us, length us, event | category | flops | bytes accessed | tf_op | source)
XLA Modules:
  0.0 281.3 jit_solution(13004928788901511606)
XLA Ops:
  3.0 47.9 %all_gather.3 = f32[32,6,1152]{2,1,0:T(8,128)} all-gather(f32[1,6,1152]{2,1,0:T(8,128)S(1)} %copy.83), channel_id=1, replica_groups=mesh['dp'=32,'seq'=8] {'dp'}, dimensions={0}, use_global_device_ids=true | all-gather | bytes 912384 | tf_op jit(solution)/shard_map/all_gather | solution.py:87
  50.9 2.6 gather_fusion
  57.9 5.4 %convolution_convert_fusion = bf16[832,1728]{1,0:T(8,128)(2,1)} fusion(bf16[832,1152]{1,0:T(8,128)(2,1)S(1)} %bitcast.123, bf16[1152,1728]{0,1:T(8,128)(2,1)S(1)} %copy-done.6), kind=kOutput, calls=%fused_computation.17 | convolution fusion | flops 3313889280 | bytes 8773632 | tf_op jit(solution)/shard_map/dot_general | solution.py:46
  63.4 9.2 %reshape.348 = bf16[13,64,3,8,72]{4,3,2,1,0:T(8,128)(2,1)} reshape(bf16[832,1728]{1,0:T(8,128)(2,1)} %convolution_convert_fusion) | data formatting | bytes 5750784 | tf_op jit(solution)/shard_map/reshape | solution.py:23
  72.6 2.8 fusion.45
  76.4 5.0 %fusion.48 = (f32[13,8,64]{2,1,0:T(8,128)S(1)}, f32[13,8,64,64]{2,3,1,0:T(8,128)S(1)}) fusion(f32[13,8,64,64]{2,3,1,0:T(8,128)S(1)} %fusion.23), kind=kOutput, calls=%fused_computation.116 | output fusion | flops 1703999 | bytes 3434496 | tf_op jit(solution)/shard_map/sub | solution.py:32
  82.3 2.6 copy.88
  84.9 3.8 %dot_general.29 = bf16[13,64,576]{2,1,0:T(8,128)(2,1)} reshape(bf16[13,64,8,72]{3,2,1,0:T(8,128)(2,1)} %copy.88) | data formatting | bytes 1916928 | tf_op jit(solution)/shard_map/dot_general | solution.py:50
  88.8 4.3 %fusion.8 = bf16[13,64,1152]{2,1,0:T(8,128)(2,1)} fusion(bf16[13,64,576]{2,1,0:T(8,128)(2,1)} %dot_general.29, bf16[13,64,1152]{2,1,0:T(8,128)(2,1)S(1)} %copy-done.2, f32[13,1152]{1,0:T(8,128)S(1)} %bitcast.124, bf16[576,1152]{1,0:T(8,128)(2,1)S(1)} %copy-done), kind=kOutput, calls=%fused_computation.16 | convolution fusion | flops 1107984384 | bytes 6179328 | tf_op jit(solution)/shard_map/dot_general | solution.py:50
  93.1 4.8 %gather_fusion.1 = bf16[32,64,1152]{2,1,0:T(8,128)(2,1)} fusion(bf16[13,64,1152]{2,1,0:T(8,128)(2,1)} %fusion.8, s32[1024]{0:T(1024)S(1)} %pad_clamp_fusion.1), kind=kCustom, calls=%fused_computation.1 | custom fusion | bytes 9437312 | tf_op jit(solution)/shard_map/jit(_take)/gather | solution.py:90
  97.8 5.0 %broadcast_select_fusion = bf16[32,64,1152]{2,1,0:T(8,128)(2,1)} fusion(bf16[32,64,1152]{2,1,0:T(8,128)(2,1)} %gather_fusion.1, pred[32]{0:T(512)(128)(4,1)S(1)} %compare_and_fusion.2), kind=kLoop, calls=%fused_computation.8 | loop fusion | flops 2359296 | bytes 9437216 | tf_op jit(solution)/shard_map/jit(_take)/select_n | solution.py:90
  102.9 5.7 %all-to-all-start = ((bf16[32,64,1152]{2,1,0:T(8,128)(2,1)}), bf16[32,64,1152]{2,1,0:T(8,128)(2,1)}, u32[]{:S(2)}, u32[]{:S(2)}) async-start(bf16[32,64,1152]{2,1,0:T(8,128)(2,1)} %broadcast_select_fusion), calls=%async_computation | async-start | bytes 9437184 | tf_op jit(solution)/shard_map/all_to_all | solution.py:91
  108.8 93.4 %all-to-all-done = bf16[32,64,1152]{2,1,0:T(8,128)(2,1)} async-done(((bf16[32,64,1152]{2,1,0:T(8,128)(2,1)}), bf16[32,64,1152]{2,1,0:T(8,128)(2,1)}, u32[]{:S(2)}, u32[]{:S(2)}) %all-to-all-start) | async-done | bytes 4718624 | tf_op jit(solution)/shard_map/all_to_all | solution.py:91
  202.2 3.0 %gather_fusion.2 = bf16[7,64,1152]{2,1,0:T(8,128)(2,1)S(1)} fusion(bf16[32,64,1152]{2,1,0:T(8,128)(2,1)} %all-to-all-done, s32[1024]{0:T(1024)S(1)} %pad_clamp_fusion), kind=kCustom, calls=%fused_computation.2 | custom fusion | bytes 2064412 | tf_op jit(solution)/shard_map/jit(_take)/gather | solution.py:98
  205.3 1.3 copy_select_fusion
  206.5 18.9 %all-to-all-start.1 = ((bf16[7,8,8,1152]{3,2,0,1:T(8,128)(2,1)}), bf16[7,8,8,1152]{3,2,0,1:T(8,128)(2,1)S(1)}, u32[]{:S(2)}, u32[]{:S(2)}) async-start(bf16[7,8,8,1152]{3,2,0,1:T(8,128)(2,1)} %copy_select_fusion), calls=%async_computation.1 | async-start | bytes 2064384 | tf_op jit(solution)/shard_map/all_to_all | solution.py:105
  225.5 14.7 %all-to-all-done.1 = bf16[7,8,8,1152]{3,2,0,1:T(8,128)(2,1)S(1)} async-done(((bf16[7,8,8,1152]{3,2,0,1:T(8,128)(2,1)}), bf16[7,8,8,1152]{3,2,0,1:T(8,128)(2,1)S(1)}, u32[]{:S(2)}, u32[]{:S(2)}) %all-to-all-start.1) | async-done | bytes 1032224 | tf_op jit(solution)/shard_map/all_to_all | solution.py:105
  241.6 4.4 %fusion.15 = bf16[56,8,1728]{2,1,0:T(8,128)(2,1)S(1)} fusion(bf16[448,1152]{1,0:T(8,128)(2,1)S(1)} %fusion.19, bf16[1152,1728]{0,1:T(8,128)(2,1)} %param.14), kind=kOutput, calls=%fused_computation.27 | convolution fusion | flops 1784401920 | bytes 6561792 | tf_op jit(solution)/shard_map/dot_general | solution.py:108
  246.3 4.0 %reshape_reshape.6 = bf16[8,56,3,8,72]{4,3,2,1,0:T(8,128)(2,1)} reshape(bf16[8,56,1728]{2,1,0:T(8,128)(2,1)S(1)} %bitcast.120) | data formatting | bytes 3096576 | tf_op jit(solution)/shard_map/reshape;reshape | solution.py:23
  250.2 2.9 %fusion.46 = (bf16[8,56,1,8,72]{4,3,2,1,0:T(8,128)(2,1)S(1)}, bf16[8,56,1,8,72]{4,3,2,1,0:T(8,128)(2,1)S(1)}, bf16[8,56,1,8,72]{4,3,2,1,0:T(8,128)(2,1)}) fusion(bf16[8,56,3,8,72]{4,3,2,1,0:T(8,128)(2,1)} %reshape_reshape.6), kind=kLoop, calls=%fused_computation.114 | loop fusion | bytes 3096576 | tf_op jit(solution)/shard_map/slice | solution.py:35
  253.1 3.5 %fusion.49 = (f32[8,8,56]{2,1,0:T(8,128)S(1)}, f32[8,8,56,56]{2,3,1,0:T(8,128)}) fusion(bf16[8,56,1,8,72]{4,3,2,1,0:T(8,128)(2,1)} %get-tuple-element.15, bf16[8,56,1,8,72]{4,3,2,1,0:T(8,128)(2,1)S(1)} %get-tuple-element.14), kind=kOutput, calls=%fused_computation.117 | convolution fusion | flops 29503544 | bytes 1849344 | tf_op jit(solution)/shard_map/sub | solution.py:32
  256.6 2.2 fusion.27
  259.8 1.2 copy-done.3
  262.0 18.2 %all_to_all.29 = bf16[56,1,8,1152]{3,2,1,0:T(8,128)(2,1)S(1)} all-to-all(bf16[56,1,8,1152]{3,2,1,0:T(8,128)(2,1)S(1)} %fusion.14), channel_id=1, replica_groups=mesh['dp'=32,'seq'=8] {'seq'}, dimensions={0} | all-to-all | bytes 2064384 | tf_op jit(solution)/shard_map/all_to_all | solution.py:129
  (59 shorter events, 14.1 us)
Async XLA Ops:
  0.0 88.8 %copy-start = (bf16[576,1152]{1,0:T(8,128)(2,1)S(1)}, bf16[576,1152]{1,0:T(8,128)(2,1)}, u32[]{:S(2)}) copy-start(bf16[576,1152]{1,0:T(8,128)(2,1)} %param.13) | copy-start | bytes 3981316
  0.0 54.8 %copy-start.2 = (bf16[13,64,1152]{2,1,0:T(8,128)(2,1)S(1)}, bf16[13,64,1152]{2,1,0:T(8,128)(2,1)}, u32[]{:S(2)}) copy-start(bf16[13,64,1152]{2,1,0:T(8,128)(2,1)} %param.8) | copy-start | bytes 5750788
  55.8 2.1 copy-start.6
  102.9 5.7 %copy-start.5 = (s32[32,13]{0,1:T(8,128)S(1)}, s32[32,13]{0,1:T(8,128)}, u32[]{:S(2)}) copy-start(s32[32,13]{0,1:T(8,128)} %param.11) | copy-start | bytes 4996
  102.9 99.3 %all-to-all-start = ((bf16[32,64,1152]{2,1,0:T(8,128)(2,1)}), bf16[32,64,1152]{2,1,0:T(8,128)(2,1)}, u32[]{:S(2)}, u32[]{:S(2)}) async-start(bf16[32,64,1152]{2,1,0:T(8,128)(2,1)} %broadcast_select_fusion), calls=%async_computation | async-start | bytes 9437184 | tf_op jit(solution)/shard_map/all_to_all | solution.py:91
  205.2 20.2 %copy-start.4 = (f32[1,6,1152]{2,0,1:T(1,128)S(1)}, f32[1,6,1152]{2,0,1:T(1,128)}, u32[]{:S(2)}) copy-start(f32[1,6,1152]{2,0,1:T(1,128)} %param.9) | copy-start | bytes 82948
  206.5 33.7 %all-to-all-start.1 = ((bf16[7,8,8,1152]{3,2,0,1:T(8,128)(2,1)}), bf16[7,8,8,1152]{3,2,0,1:T(8,128)(2,1)S(1)}, u32[]{:S(2)}, u32[]{:S(2)}) async-start(bf16[7,8,8,1152]{3,2,0,1:T(8,128)(2,1)} %copy_select_fusion), calls=%async_computation.1 | async-start | bytes 2064384 | tf_op jit(solution)/shard_map/all_to_all | solution.py:105
  259.6 1.3 copy-start.3
  261.0 20.3 %copy-start.1 = (bf16[576,1152]{1,0:T(8,128)(2,1)S(1)}, bf16[576,1152]{1,0:T(8,128)(2,1)}, u32[]{:S(2)}) copy-start(bf16[576,1152]{1,0:T(8,128)(2,1)} %param.13) | copy-start | bytes 3981316
where the time goes:
time: 282 us; the launch traced here: 281 us
  waiting for transfers between devices  108 us (38%)
  blocking collectives  66.1 us (23%)
  local copies, waits for them, and re-layouts  41.4 us (15%)
  starting transfers between devices  24.6 us (9%)
  matrix products  22.7 us (8%)
  other arithmetic  18.1 us (6%)
    all_to_all x1, waiting for transfers between devices, on_device(): lax.all_to_all(payload, 'dp', split_axis=0, concat_axis=0, tiled=True)  93.4 us
    all_gather x1, blocking collectives, on_device(): video_rows = lax.all_gather(modulation, 'dp', axis=0, tiled=True)  47.9 us
    all_to_all x1, starting transfers between devices, on_device(): lax.all_to_all(selected, 'seq', split_axis=1, concat_axis=0, tiled=True)  18.9 us
    all_to_all x1, blocking collectives, on_device(): lax.all_to_all(homeward.reshape(frame_total, 1, widest, back_width), 'seq...  18.2 us
    all_to_all x1, waiting for transfers between devices, on_device(): lax.all_to_all(selected, 'seq', split_axis=1, concat_axis=0, tiled=True)  14.7 us
    reshape x1, local copies, waits for them, and re-layouts, attention(): parts = qkv_rows.reshape(batch_count, length, 3, HEADS, HEAD_DIM)  9.25 us
    all_to_all x1, starting transfers between devices, on_device(): lax.all_to_all(payload, 'dp', split_axis=0, concat_axis=0, tiled=True)  5.69 us
    slice x2, local copies, waits for them, and re-layouts, attention(): parts[:, :, 2]  5.66 us
  transfers between devices with their start and end apart: 2, of which 2 were waited for; matrix products, arithmetic and copies ran while one was open for 0% of the time, Pallas kernels for 0%

commit v1 on v0

--- a/solution.py
+++ b/solution.py
@@ -84,7 +84,10 @@
         & (own_rank[:, None, None] == room_ids[None, None, :])
     )
     chosen_slot = jnp.sum(picks.astype(jnp.int32) * slot_ids[:, None, None], axis=0).reshape(-1)
-    video_rows = lax.all_gather(modulation, "dp", axis=0, tiled=True)
+    size = lax.axis_size("dp")
+    tiles = jnp.stack([modulation for _ in range(size)])
+    tiles = lax.all_to_all(tiles, "dp", split_axis=0, concat_axis=0)
+    video_rows = jnp.concatenate(tiles, axis=0)
     slot_modulation = jnp.take(video_rows, own_target, axis=0)
     processed = spatial_block(slot_tokens, slot_modulation, qkv_spatial, out_spatial)
     payload = jnp.take(processed, chosen_slot, axis=0)

time: 282 us -> 270 us (0.957)
  blocking collectives: 66.1 us -> 18.2 us
  waiting for transfers between devices: 108 us -> 139 us
  local copies, waits for them, and re-layouts: 41.4 us -> 45.2 us
    all_gather x1 -> x0, blocking collectives: 47.9 us -> none  [on_device(): video_rows = lax.all_gather(modulation, 'dp', axis=0, tiled=True)]
    all_to_all x0 -> x1, waiting for transfers between devices: none -> 21.2 us  [on_device(): tiles = lax.all_to_all(tiles, 'dp', split_axis=0, concat_axis=0)]
    all_to_all x0 -> x1, starting transfers between devices: none -> 12.1 us  [on_device(): tiles = lax.all_to_all(tiles, 'dp', split_axis=0, concat_axis=0)]
    all_to_all x1, starting transfers between devices: 18.9 us -> 6.99 us  [on_device(): lax.all_to_all(selected, 'seq', split_axis=1, concat_axis=0, tiled=True)]
    all_to_all x1, waiting for transfers between devices: 93.4 us -> 103 us  [on_device(): lax.all_to_all(payload, 'dp', split_axis=0, concat_axis=0, tiled=True)]
  transfers between devices with their start and end apart: 2 -> 3, of which waited for: 2 -> 3; matrix products, arithmetic and copies ran while one was open for 0% -> 1% of each run, Pallas kernels for 0% -> 0%
where the time goes in v1:
time: 270 us; the launch traced here: 268 us
  waiting for transfers between devices  139 us (51%)
  local copies, waits for them, and re-layouts  45.2 us (17%)
  starting transfers between devices  25.2 us (9%)
  matrix products  22.7 us (8%)
  blocking collectives  18.2 us (7%)
  other arithmetic  16.6 us (6%)
    all_to_all x1, waiting for transfers between devices, on_device(): lax.all_to_all(payload, 'dp', split_axis=0, concat_axis=0, tiled=True)  103 us
    all_to_all x1, waiting for transfers between devices, on_device(): tiles = lax.all_to_all(tiles, 'dp', split_axis=0, concat_axis=0)  21.2 us
    all_to_all x1, blocking collectives, on_device(): lax.all_to_all(homeward.reshape(frame_total, 1, widest, back_width), 'seq...  18.2 us
    all_to_all x1, waiting for transfers between devices, on_device(): lax.all_to_all(selected, 'seq', split_axis=1, concat_axis=0, tiled=True)  14.7 us
    all_to_all x1, starting transfers between devices, on_device(): tiles = lax.all_to_all(tiles, 'dp', split_axis=0, concat_axis=0)  12.1 us
    reshape x1, local copies, waits for them, and re-layouts, attention(): parts = qkv_rows.reshape(batch_count, length, 3, HEADS, HEAD_DIM)  9.25 us
    all_to_all x1, starting transfers between devices, on_device(): lax.all_to_all(selected, 'seq', split_axis=1, concat_axis=0, tiled=True)  6.99 us
    all_to_all x1, starting transfers between devices, on_device(): lax.all_to_all(payload, 'dp', split_axis=0, concat_axis=0, tiled=True)  6.09 us
  transfers between devices with their start and end apart: 3, of which 3 were waited for; matrix products, arithmetic and copies ran while one was open for 1% of the time, Pallas kernels for 0%

profile of v1, /device:TPU:1, one launch (start us, length us, event | category | flops | bytes accessed | tf_op | source)
XLA Modules:
  0.0 267.6 jit_solution(4942180043503981817)
XLA Ops:
  2.3 12.1 %all-to-all-start = ((f32[32,1,6,1152]{3,1,2,0:T(1,128)}), f32[32,1,6,1152]{3,1,2,0:T(1,128)}, u32[]{:S(2)}, u32[]{:S(2)}) async-start(f32[32,1,6,1152]{3,1,2,0:T(1,128)} %stack.2), calls=%async_computation | async-start | bytes 1769472 | tf_op jit(solution)/shard_map/all_to_all | solution.py:89
  16.2 21.2 %all-to-all-done = f32[32,1,6,1152]{3,1,2,0:T(1,128)} async-done(((f32[32,1,6,1152]{3,1,2,0:T(1,128)}), f32[32,1,6,1152]{3,1,2,0:T(1,128)}, u32[]{:S(2)}, u32[]{:S(2)}) %all-to-all-start) | async-done | bytes 884768 | tf_op jit(solution)/shard_map/all_to_all | solution.py:89
  37.4 2.3 copy.193
  39.7 2.6 gather_fusion
  45.7 5.4 %convolution_convert_fusion = bf16[832,1728]{1,0:T(8,128)(2,1)} fusion(bf16[832,1152]{1,0:T(8,128)(2,1)S(1)} %bitcast.131, bf16[1152,1728]{0,1:T(8,128)(2,1)S(1)} %copy-done.7), kind=kOutput, calls=%fused_computation.17 | convolution fusion | flops 3313889280 | bytes 8773632 | tf_op jit(solution)/shard_map/dot_general | solution.py:46
  51.2 9.2 %reshape.355 = bf16[13,64,3,8,72]{4,3,2,1,0:T(8,128)(2,1)} reshape(bf16[832,1728]{1,0:T(8,128)(2,1)} %convolution_convert_fusion) | data formatting | bytes 5750784 | tf_op jit(solution)/shard_map/reshape | solution.py:23
  60.4 2.8 %fusion.45 = (bf16[13,64,1,8,72]{4,3,2,1,0:T(8,128)(2,1)S(1)}, bf16[13,64,1,8,72]{4,3,2,1,0:T(8,128)(2,1)S(1)}, bf16[13,64,1,8,72]{4,3,2,1,0:T(8,128)(2,1)S(1)}) fusion(bf16[13,64,3,8,72]{4,3,2,1,0:T(8,128)(2,1)} %reshape.355), kind=kLoop, calls=%fused_computation.115 | loop fusion | bytes 5750784 | tf_op jit(solution)/shard_map/slice | solution.py:35
  64.2 5.0 %fusion.48 = (f32[13,8,64]{2,1,0:T(8,128)S(1)}, f32[13,8,64,64]{2,3,1,0:T(8,128)S(1)}) fusion(f32[13,8,64,64]{2,3,1,0:T(8,128)S(1)} %fusion.23), kind=kOutput, calls=%fused_computation.118 | output fusion | flops 1703999 | bytes 3434496 | tf_op jit(solution)/shard_map/sub | solution.py:32
  70.1 2.6 copy.113
  72.7 3.8 %dot_general.29 = bf16[13,64,576]{2,1,0:T(8,128)(2,1)} reshape(bf16[13,64,8,72]{3,2,1,0:T(8,128)(2,1)} %copy.113) | data formatting | bytes 1916928 | tf_op jit(solution)/shard_map/dot_general | solution.py:50
  76.6 4.3 %fusion.8 = bf16[13,64,1152]{2,1,0:T(8,128)(2,1)} fusion(bf16[13,64,576]{2,1,0:T(8,128)(2,1)} %dot_general.29, bf16[13,64,1152]{2,1,0:T(8,128)(2,1)S(1)} %copy-done.2, f32[13,1152]{1,0:T(8,128)S(1)} %bitcast.133, bf16[576,1152]{1,0:T(8,128)(2,1)S(1)} %copy-done), kind=kOutput, calls=%fused_computation.16 | convolution fusion | flops 1107984384 | bytes 6179328 | tf_op jit(solution)/shard_map/dot_general | solution.py:50
  80.8 4.8 %gather_fusion.1 = bf16[32,64,1152]{2,1,0:T(8,128)(2,1)} fusion(bf16[13,64,1152]{2,1,0:T(8,128)(2,1)} %fusion.8, s32[1024]{0:T(1024)S(1)} %pad_clamp_fusion.1), kind=kCustom, calls=%fused_computation.1 | custom fusion | bytes 9437312 | tf_op jit(solution)/shard_map/jit(_take)/gather | solution.py:93
  85.6 5.0 %broadcast_select_fusion = bf16[32,64,1152]{2,1,0:T(8,128)(2,1)} fusion(bf16[32,64,1152]{2,1,0:T(8,128)(2,1)} %gather_fusion.1, pred[32]{0:T(512)(128)(4,1)S(1)} %compare_and_fusion.2), kind=kLoop, calls=%fused_computation.8 | loop fusion | flops 2359296 | bytes 9437216 | tf_op jit(solution)/shard_map/jit(_take)/select_n | solution.py:93
  90.6 6.1 %all-to-all-start.1 = ((bf16[32,64,1152]{2,1,0:T(8,128)(2,1)}), bf16[32,64,1152]{2,1,0:T(8,128)(2,1)}, u32[]{:S(2)}, u32[]{:S(2)}) async-start(bf16[32,64,1152]{2,1,0:T(8,128)(2,1)} %broadcast_select_fusion), calls=%async_computation.1 | async-start | bytes 9437184 | tf_op jit(solution)/shard_map/all_to_all | solution.py:94
  97.0 103.4 %all-to-all-done.1 = bf16[32,64,1152]{2,1,0:T(8,128)(2,1)} async-done(((bf16[32,64,1152]{2,1,0:T(8,128)(2,1)}), bf16[32,64,1152]{2,1,0:T(8,128)(2,1)}, u32[]{:S(2)}, u32[]{:S(2)}) %all-to-all-start.1) | async-done | bytes 4718624 | tf_op jit(solution)/shard_map/all_to_all | solution.py:94
  200.4 3.0 %gather_fusion.2 = bf16[7,64,1152]{2,1,0:T(8,128)(2,1)S(1)} fusion(bf16[32,64,1152]{2,1,0:T(8,128)(2,1)} %all-to-all-done.1, s32[1024]{0:T(1024)S(1)} %pad_clamp_fusion), kind=kCustom, calls=%fused_computation.2 | custom fusion | bytes 2064412 | tf_op jit(solution)/shard_map/jit(_take)/gather | solution.py:101
  204.7 7.0 %all-to-all-start.2 = ((bf16[7,8,8,1152]{3,2,0,1:T(8,128)(2,1)}), bf16[7,8,8,1152]{3,2,0,1:T(8,128)(2,1)S(1)}, u32[]{:S(2)}, u32[]{:S(2)}) async-start(bf16[7,8,8,1152]{3,2,0,1:T(8,128)(2,1)} %copy_select_fusion), calls=%async_computation.2 | async-start | bytes 2064384 | tf_op jit(solution)/shard_map/all_to_all | solution.py:108
  211.8 14.7 %all-to-all-done.2 = bf16[7,8,8,1152]{3,2,0,1:T(8,128)(2,1)S(1)} async-done(((bf16[7,8,8,1152]{3,2,0,1:T(8,128)(2,1)}), bf16[7,8,8,1152]{3,2,0,1:T(8,128)(2,1)S(1)}, u32[]{:S(2)}, u32[]{:S(2)}) %all-to-all-start.2) | async-done | bytes 1032224 | tf_op jit(solution)/shard_map/all_to_all | solution.py:108
  227.9 4.4 %fusion.15 = bf16[56,8,1728]{2,1,0:T(8,128)(2,1)S(1)} fusion(bf16[448,1152]{1,0:T(8,128)(2,1)S(1)} %fusion.19, bf16[1152,1728]{0,1:T(8,128)(2,1)} %param.14), kind=kOutput, calls=%fused_computation.27 | convolution fusion | flops 1784401920 | bytes 6561792 | tf_op jit(solution)/shard_map/dot_general | solution.py:111
  232.5 4.0 %reshape_reshape.6 = bf16[8,56,3,8,72]{4,3,2,1,0:T(8,128)(2,1)} reshape(bf16[8,56,1728]{2,1,0:T(8,128)(2,1)S(1)} %bitcast.127) | data formatting | bytes 3096576 | tf_op jit(solution)/shard_map/reshape;reshape | solution.py:23
  236.5 2.9 %fusion.46 = (bf16[8,56,1,8,72]{4,3,2,1,0:T(8,128)(2,1)S(1)}, bf16[8,56,1,8,72]{4,3,2,1,0:T(8,128)(2,1)S(1)}, bf16[8,56,1,8,72]{4,3,2,1,0:T(8,128)(2,1)}) fusion(bf16[8,56,3,8,72]{4,3,2,1,0:T(8,128)(2,1)} %reshape_reshape.6), kind=kLoop, calls=%fused_computation.116 | loop fusion | bytes 3096576 | tf_op jit(solution)/shard_map/slice | solution.py:35
  239.4 3.5 %fusion.49 = (f32[8,8,56]{2,1,0:T(8,128)S(1)}, f32[8,8,56,56]{2,3,1,0:T(8,128)}) fusion(bf16[8,56,1,8,72]{4,3,2,1,0:T(8,128)(2,1)} %get-tuple-element.15, bf16[8,56,1,8,72]{4,3,2,1,0:T(8,128)(2,1)S(1)} %get-tuple-element.14), kind=kOutput, calls=%fused_computation.119 | convolution fusion | flops 29503544 | bytes 1849344 | tf_op jit(solution)/shard_map/sub | solution.py:32
  242.9 2.2 fusion.27
  248.3 18.2 %all_to_all.34 = bf16[56,1,8,1152]{3,2,1,0:T(8,128)(2,1)S(1)} all-to-all(bf16[56,1,8,1152]{3,2,1,0:T(8,128)(2,1)S(1)} %fusion.14), channel_id=1, replica_groups=mesh['dp'=32,'seq'=8] {'seq'}, dimensions={0} | all-to-all | bytes 2064384 | tf_op jit(solution)/shard_map/all_to_all | solution.py:132
  (64 shorter events, 16.6 us)
Async XLA Ops:
  0.0 76.6 %copy-start = (bf16[576,1152]{1,0:T(8,128)(2,1)S(1)}, bf16[576,1152]{1,0:T(8,128)(2,1)}, u32[]{:S(2)}) copy-start(bf16[576,1152]{1,0:T(8,128)(2,1)} %param.13) | copy-start | bytes 3981316
  0.0 14.5 %copy-start.5 = (s32[32,13]{0,1:T(8,128)S(1)}, s32[32,13]{0,1:T(8,128)}, u32[]{:S(2)}) copy-start(s32[32,13]{0,1:T(8,128)} %param.11) | copy-start | bytes 4996
  0.0 14.7 %copy-start.6 = (s32[32]{0:T(128)S(1)}, s32[32]{0:T(128)}, u32[]{:S(2)}) copy-start(s32[32]{0:T(128)} %param.10) | copy-start | bytes 388
  0.0 15.2 %copy-start.2 = (bf16[13,64,1152]{2,1,0:T(8,128)(2,1)S(1)}, bf16[13,64,1152]{2,1,0:T(8,128)(2,1)}, u32[]{:S(2)}) copy-start(bf16[13,64,1152]{2,1,0:T(8,128)(2,1)} %param.8) | copy-start | bytes 5750788
  2.3 35.1 %all-to-all-start = ((f32[32,1,6,1152]{3,1,2,0:T(1,128)}), f32[32,1,6,1152]{3,1,2,0:T(1,128)}, u32[]{:S(2)}, u32[]{:S(2)}) async-start(f32[32,1,6,1152]{3,1,2,0:T(1,128)} %stack.2), calls=%async_computation | async-start | bytes 1769472 | tf_op jit(solution)/shard_map/all_to_all | solution.py:89
  43.6 2.1 copy-start.7
  90.6 109.7 %all-to-all-start.1 = ((bf16[32,64,1152]{2,1,0:T(8,128)(2,1)}), bf16[32,64,1152]{2,1,0:T(8,128)(2,1)}, u32[]{:S(2)}, u32[]{:S(2)}) async-start(bf16[32,64,1152]{2,1,0:T(8,128)(2,1)} %broadcast_select_fusion), calls=%async_computation.1 | async-start | bytes 9437184 | tf_op jit(solution)/shard_map/all_to_all | solution.py:94
  203.4 8.3 %copy-start.4 = (f32[1,6,1152]{2,0,1:T(1,128)S(1)}, f32[1,6,1152]{2,0,1:T(1,128)}, u32[]{:S(2)}) copy-start(f32[1,6,1152]{2,0,1:T(1,128)} %param.9) | copy-start | bytes 82948
  204.7 21.8 %all-to-all-start.2 = ((bf16[7,8,8,1152]{3,2,0,1:T(8,128)(2,1)}), bf16[7,8,8,1152]{3,2,0,1:T(8,128)(2,1)S(1)}, u32[]{:S(2)}, u32[]{:S(2)}) async-start(bf16[7,8,8,1152]{3,2,0,1:T(8,128)(2,1)} %copy_select_fusion), calls=%async_computation.2 | async-start | bytes 2064384 | tf_op jit(solution)/shard_map/all_to_all | solution.py:108
  245.9 1.3 copy-start.3
  247.2 20.3 %copy-start.1 = (bf16[576,1152]{1,0:T(8,128)(2,1)S(1)}, bf16[576,1152]{1,0:T(8,128)(2,1)}, u32[]{:S(2)}) copy-start(bf16[576,1152]{1,0:T(8,128)(2,1)} %param.13) | copy-start | bytes 3981316
